TPU v7x, 256 devices: a whole 4x4x8 slice. The times are simulated.
256 devices in a mesh: row: 16 (over y_lo, x, core), col: 16 (over z, y_hi).
Axes of the slice: x: 4, y: 4 (y_hi: 2, y_lo: 2; y = y_hi * 2 + y_lo), z: 8, core: 2. Of those that a mesh axis runs over, the one named last changes fastest.
Arguments:
- counts: int32 [16, 16, 6, 8, 128, 128], P('row', 'col'), may hold values from 0 to 5
- block_coords: int32 [3, 16, 16, 6], P(None, 'row', 'col'), may hold values from 0 to 127, as said below
- block_count: int32 [16, 16], P('row', 'col'), may hold values from 1 to 6, as said below
- factor_a: float32 [32768, 128], P(('row', 'col')), may hold values from -0.6 to 0.6
- factor_b: float32 [32768, 128], P(('col', 'row')), may hold values from -0.6 to 0.6
- factor_c: float32 [1024, 128], replicated, may hold values from -0.6 to 0.6
Outputs:
- updated_a: float32 [32768, 128], P(('row', 'col'))
- updated_b: float32 [32768, 128], P(('col', 'row'))
Inputs may be any that keep to these rules, and one draw needn't show every extreme that they name: `block_coords`: the slots of one cell name distinct blocks; the first index is below 16, the second below 16, the third below 128. `block_count`: at least one cell has all 6 slots live in every draw.
All inputs are finite; a program needn't handle non-finite values.
Results may differ from a plain program's by a relative error of at most 0.0003.
Values sent between devices are 32-bit elements; how exact they have to be, the bound alone decides.
No kernel may reach another device: no remote copies, remote signals or barrier semaphores. Data moves between devices by JAX's collectives and lax.ppermute only.
A program may use at most 64 MiB of HBM per device.

v0:
```python
import jax
import jax.numpy as jnp
from jax import lax
from jax.sharding import PartitionSpec as P

STEPS = 2
step_rate = 0.004
highest = lax.Precision.HIGHEST


def block_gradient(piece_a, piece_b, piece_c, observed, valid_flag):
    depth = piece_c.shape[0]
    side = piece_a.shape[0]
    rank = piece_a.shape[1]
    scaled_a = (piece_c[:, None, :] * piece_a[None, :, :]).reshape(depth * side, rank)
    model = jnp.dot(scaled_a, piece_b.T, precision=highest, preferred_element_type=jnp.float32)
    residual = (
        jnp.exp(model) - observed.reshape(depth * side, side).astype(jnp.float32)
    ) * valid_flag
    scaled_b = piece_c[:, None, :] * piece_b[None, :, :]
    grad_a = jnp.einsum(
        "kab,kbr->ar", residual.reshape(depth, side, side), scaled_b, precision=highest
    )
    grad_b = jnp.dot(residual.T, scaled_a, precision=highest, preferred_element_type=jnp.float32)
    return (grad_a, grad_b)


def local_gradients(band_a, band_b, factor_c, counts, block_coords, block_count):
    slot_total = counts.shape[2]
    depth = counts.shape[3]
    side = counts.shape[4]
    limit = block_count[0, 0]

    def visit_slot(partial_value, slot_index):
        grad_a, grad_b = partial_value
        start_a = block_coords[0, 0, 0, slot_index] * side
        start_b = block_coords[1, 0, 0, slot_index] * side
        start_c = block_coords[2, 0, 0, slot_index] * depth
        valid_flag = (slot_index < limit).astype(jnp.float32)
        piece_a = lax.dynamic_slice_in_dim(band_a, start_a, side, 0)
        piece_b = lax.dynamic_slice_in_dim(band_b, start_b, side, 0)
        piece_c = lax.dynamic_slice_in_dim(factor_c, start_c, depth, 0)
        observed = counts[0, 0, slot_index]
        block_a, block_b = block_gradient(piece_a, piece_b, piece_c, observed, valid_flag)
        old_a = lax.dynamic_slice_in_dim(grad_a, start_a, side, 0)
        old_b = lax.dynamic_slice_in_dim(grad_b, start_b, side, 0)
        grad_a = lax.dynamic_update_slice_in_dim(grad_a, old_a + block_a, start_a, 0)
        grad_b = lax.dynamic_update_slice_in_dim(grad_b, old_b + block_b, start_b, 0)
        return ((grad_a, grad_b), None)

    start = (jnp.zeros_like(band_a), jnp.zeros_like(band_b))
    result, unused = lax.scan(visit_slot, start, jnp.arange(slot_total, dtype=jnp.int32))
    return result


def local(counts, block_coords, block_count, factor_a, factor_b, factor_c):
    for step_index in range(STEPS):
        band_a = lax.all_gather(factor_a, "col", axis=0, tiled=True)
        band_b = lax.all_gather(factor_b, "row", axis=0, tiled=True)
        grad_a, grad_b = local_gradients(
            band_a, band_b, factor_c, counts, block_coords, block_count
        )
        share_a = lax.psum_scatter(grad_a, "col", scatter_dimension=0, tiled=True)
        share_b = lax.psum_scatter(grad_b, "row", scatter_dimension=0, tiled=True)
        factor_a = factor_a - step_rate * share_a
        factor_b = factor_b - step_rate * share_b
    return (factor_a, factor_b)


def solution(mesh):
    return jax.shard_map(
        local,
        mesh=mesh,
        in_specs=(
            P("row", "col", None, None, None, None),
            P(None, "row", "col", None),
            P("row", "col"),
            P(("row", "col"), None),
            P(("col", "row"), None),
            P(),
        ),
        out_specs=(P(("row", "col"), None), P(("col", "row"), None)),
        check_vma=False,
    )
```

profile of v0, /device:TPU:4, one launch (start us, length us, event | category | flops | bytes accessed | tf_op | source)
XLA Modules:
  0.0 932.4 jit_solution(7172400108618782772)
XLA Ops:
  8.7 83.6 %all-gather.5.cloned.1.call-done = f32[2048,128]{1,0:T(8,128)} async-done(((f32[128,128]{1,0:T(8,128)}), f32[2048,128]{1,0:T(8,128)}) %all-gather.5.cloned.1.call-update) | async-done | bytes 1048592 | tf_op jit(solution)/shard_map/all_gather | solution.py:58
  92.3 32.1 %all-gather.7.cloned.1.call-done = f32[2048,128]{1,0:T(8,128)} async-done(((f32[128,128]{1,0:T(8,128)}), f32[2048,128]{1,0:T(8,128)}) %all-gather.7.cloned.1.call-update) | async-done | bytes 1048592 | tf_op jit(solution)/shard_map/all_gather | solution.py:59
  124.6 71.9 %while.24 = (s32[]{:T(128)}, f32[2048,128]{1,0:T(8,128)S(1)}, f32[2048,128]{1,0:T(8,128)S(1)}, s32[6]{0:T(128)S(1)}, s32[3,1,1,6]{3,2,1,0:T(1,128)}, /*index=5*/...) while((s32[]{:T(128)}, f32[2048,128]{1,0:T(8,128)S(1)}, ...), condition=%wide.region_1.2_spmd, body=%wide.region_0.1_spmd.sunk | while | flops 604667904 | bytes 5456283 | solution.py:52
  127.1 1.3 constant_dynamic-slice_fusion.18
  131.9 1.1 dynamic-slice_convert_fusion.4
  139.1 1.3 constant_dynamic-slice_fusion.18
  143.9 1.1 dynamic-slice_convert_fusion.4
  151.1 1.3 constant_dynamic-slice_fusion.18
  163.1 1.3 constant_dynamic-slice_fusion.18
  175.1 1.3 constant_dynamic-slice_fusion.18
  187.1 1.3 constant_dynamic-slice_fusion.18
  198.2 58.2 %reduce-scatter.7.cloned.1.call-done = f32[128,128]{1,0:T(8,128)} async-done(((f32[2048,128]{1,0:T(8,128)}), f32[128,128]{1,0:T(8,128)}) %reduce-scatter.7.cloned.1.call-update) | async-done | bytes 65552 | tf_op jit(solution)/shard_map/reduce_scatter | solution.py:64
  256.4 1.5 multiply_subtract_fusion.2
  258.0 211.8 %reduce-scatter.5.cloned.1.call-done = f32[128,128]{1,0:T(8,128)} async-done(((f32[2048,128]{1,0:T(8,128)}), f32[128,128]{1,0:T(8,128)}) %reduce-scatter.5.cloned.1.call-update) | async-done | bytes 65552 | tf_op jit(solution)/shard_map/reduce_scatter | solution.py:63
  469.8 1.5 multiply_subtract_fusion.3
  471.4 32.5 %all-gather.11.cloned.1.call-done = f32[2048,128]{1,0:T(8,128)} async-done(((f32[128,128]{1,0:T(8,128)}), f32[2048,128]{1,0:T(8,128)}) %all-gather.11.cloned.1.call-update) | async-done | bytes 1048592 | tf_op jit(solution)/shard_map/all_gather | solution.py:59
  503.9 82.6 %all-gather.9.cloned.1.call-done = f32[2048,128]{1,0:T(8,128)} async-done(((f32[128,128]{1,0:T(8,128)}), f32[2048,128]{1,0:T(8,128)}) %all-gather.9.cloned.1.call-update) | async-done | bytes 1048592 | tf_op jit(solution)/shard_map/all_gather | solution.py:58
  586.7 68.0 %while.25 = (s32[]{:T(128)}, f32[2048,128]{1,0:T(8,128)S(1)}, f32[2048,128]{1,0:T(8,128)S(1)}, s32[6]{0:T(128)S(1)}, s32[3,1,1,6]{3,2,1,0:T(1,128)S(1)}, /*index...) while((s32[]{:T(128)}, f32[2048,128]{1,0:T(8,128)S(1)}, ...), condition=%wide.region_5.6_spmd, body=%wide.region_4.5_spmd.sunk | while | flops 604667904 | bytes 5456283 | solution.py:52
  627.4 1.1 dynamic-slice_convert_fusion.5
  638.7 1.1 dynamic-slice_convert_fusion.5
  656.5 53.7 %reduce-scatter.11.cloned.1.call-done = f32[128,128]{1,0:T(8,128)} async-done(((f32[2048,128]{1,0:T(8,128)}), f32[128,128]{1,0:T(8,128)}) %reduce-scatter.11.cloned.1.call-update) | async-done | bytes 65552 | tf_op jit(solution)/shard_map/reduce_scatter | solution.py:64
  710.2 1.5 multiply_subtract_fusion
  711.7 212.4 %reduce-scatter.9.cloned.1.call-done = f32[128,128]{1,0:T(8,128)} async-done(((f32[2048,128]{1,0:T(8,128)}), f32[128,128]{1,0:T(8,128)}) %reduce-scatter.9.cloned.1.call-update) | async-done | bytes 65552 | tf_op jit(solution)/shard_map/reduce_scatter | solution.py:63
  924.1 1.5 multiply_subtract_fusion.1
  (138 shorter events, 72.0 us)
Async XLA Ops:
  7.2 85.1 %all-gather.5.cloned.1.call-start = ((), (), s32[]{:S(2)}) async-start(), calls=%async_computation.4 | async-start | bytes 1114112 | tf_op jit(solution)/shard_map/all_gather | solution.py:58
  7.9 116.5 %all-gather.7.cloned.1.call-start = ((), (), s32[]{:S(2)}) async-start(), calls=%async_computation.5 | async-start | bytes 1114112 | tf_op jit(solution)/shard_map/all_gather | solution.py:59
  8.6 247.8 %reduce-scatter.7.cloned.1.call-start = ((), (), s32[]{:S(2)}) async-start(), calls=%async_computation.8 | async-start | bytes 1114112 | tf_op jit(solution)/shard_map/reduce_scatter | solution.py:64
  124.5 131.9 %copy-start.6 = (f32[128,128]{1,0:T(8,128)S(1)}, f32[128,128]{1,0:T(8,128)}, u32[]{:S(2)}) copy-start(f32[128,128]{1,0:T(8,128)} %param.14) | copy-start | bytes 196612
  124.6 345.2 %copy-start.7 = (f32[128,128]{1,0:T(8,128)S(1)}, f32[128,128]{1,0:T(8,128)}, u32[]{:S(2)}) copy-start(f32[128,128]{1,0:T(8,128)} %param.13) | copy-start | bytes 196612
  196.5 1.0 copy-start.3
  196.5 1.3 copy-start.2
  196.5 390.1 %copy-start.8 = (s32[3,1,1,6]{3,2,1,0:T(1,128)S(1)}, s32[3,1,1,6]{3,2,1,0:T(1,128)}, u32[]{:S(2)}) copy-start(s32[3,1,1,6]{3,2,1,0:T(1,128)} %get-tuple-element.431) | copy-start | bytes 220
  197.6 272.2 %reduce-scatter.5.cloned.1.call-start = ((), (), s32[]{:S(2)}) async-start(), calls=%async_computation.6 | async-start | bytes 1114112 | tf_op jit(solution)/shard_map/reduce_scatter | solution.py:63
  198.1 305.8 %all-gather.11.cloned.1.call-start = ((), (), s32[]{:S(2)}) async-start(), calls=%async_computation.9 | async-start | bytes 1114112 | tf_op jit(solution)/shard_map/all_gather | solution.py:59
  258.0 328.6 %all-gather.9.cloned.1.call-start = ((), (), s32[]{:S(2)}) async-start(), calls=%async_computation.7 | async-start | bytes 1114112 | tf_op jit(solution)/shard_map/all_gather | solution.py:58
  471.3 238.9 %reduce-scatter.11.cloned.1.call-start = ((), (), s32[]{:S(2)}) async-start(), calls=%async_computation.11 | async-start | bytes 1114112 | tf_op jit(solution)/shard_map/reduce_scatter | solution.py:64
  586.7 123.5 %copy-start.4 = (f32[128,128]{1,0:T(8,128)S(1)}, f32[128,128]{1,0:T(8,128)}, u32[]{:S(2)}) copy-start(f32[128,128]{1,0:T(8,128)} %multiply_subtract_fusion.2) | copy-start | bytes 196612
  586.7 337.3 %copy-start.5 = (f32[128,128]{1,0:T(8,128)S(1)}, f32[128,128]{1,0:T(8,128)}, u32[]{:S(2)}) copy-start(f32[128,128]{1,0:T(8,128)} %multiply_subtract_fusion.3) | copy-start | bytes 196612
  654.7 0.9 copy-start.1
  654.8 1.3 copy-start
  655.7 268.3 %reduce-scatter.9.cloned.1.call-start = ((), (), s32[]{:S(2)}) async-start(), calls=%async_computation.10 | async-start | bytes 1114112 | tf_op jit(solution)/shard_map/reduce_scatter | solution.py:63
Sparse Core Ops, SparseCore 0:
  10.6 81.6 all-gather.4
  94.1 30.2 all-gather.6
  197.7 58.7 reduce-scatter.6
  260.1 209.6 reduce-scatter.4
  472.1 31.7 all-gather.10
  506.9 79.5 all-gather.8
  655.8 54.2 reduce-scatter.10
  714.0 210.0 reduce-scatter.8
where the time goes:
time: 935 us; the launch traced here: 932 us
  waiting for transfers between devices  769 us (82%)
  loops' own time  61 us (7%)
  local copies, waits for them, and re-layouts  40.9 us (4%)
  matrix products  27.4 us (3%)
  other arithmetic  19.4 us (2%)
  between operations  14.3 us (2%)
    reduce_scatter x2, waiting for transfers between devices, local(): share_a = lax.psum_scatter(grad_a, 'col', scatter_dimension=0, tiled=True)  424 us
    all_gather x2, waiting for transfers between devices, local(): band_a = lax.all_gather(factor_a, 'col', axis=0, tiled=True)  166 us
    reduce_scatter x2, waiting for transfers between devices, local(): share_b = lax.psum_scatter(grad_b, 'row', scatter_dimension=0, tiled=True)  112 us
    all_gather x2, waiting for transfers between devices, local(): band_b = lax.all_gather(factor_b, 'row', axis=0, tiled=True)  64.7 us
    another operation x2, loops' own time, local_gradients(): lax.scan(visit_slot, start, jnp.arange(slot_total, dtype=jnp.int32))  61 us
  transfers between devices with their start and end apart: 8, of which 8 were waited for; matrix products, arithmetic and copies ran while one was open for 0% of the time, Pallas kernels for 0%

commit v1 on v0

--- a/solution.py
+++ b/solution.py
@@ -56,7 +56,9 @@
 def local(counts, block_coords, block_count, factor_a, factor_b, factor_c):
     for step_index in range(STEPS):
         band_a = lax.all_gather(factor_a, "col", axis=0, tiled=True)
-        band_b = lax.all_gather(factor_b, "row", axis=0, tiled=True)
+        band_b = jnp.concatenate(
+            lax.all_to_all(jnp.stack([factor_b] * lax.axis_size("row")), "row", 0, 0), axis=0
+        )
         grad_a, grad_b = local_gradients(
             band_a, band_b, factor_c, counts, block_coords, block_count
         )

time: 935 us -> 865 us (0.925)
  waiting for transfers between devices: 769 us -> 680 us
  starting transfers between devices: 0.32 us -> 17.9 us
    all_gather x2 -> x0, waiting for transfers between devices: 64.7 us -> none  [local(): band_b = lax.all_gather(factor_b, 'row', axis=0, tiled=True)]
    all_gather x2, waiting for transfers between devices: 166 us -> 129 us  [local(): band_a = lax.all_gather(factor_a, 'col', axis=0, tiled=True)]
    all_to_all x0 -> x2, waiting for transfers between devices: none -> 26.2 us  [local(): lax.all_to_all(jnp.stack([factor_b] * lax.axis_size('row')), 'row', 0, 0)]
    all_to_all x0 -> x2, starting transfers between devices: none -> 17.7 us  [local(): lax.all_to_all(jnp.stack([factor_b] * lax.axis_size('row')), 'row', 0, 0)]
    reduce_scatter x2, waiting for transfers between devices: 424 us -> 412 us  [local(): share_a = lax.psum_scatter(grad_a, 'col', scatter_dimension=0, tiled=True)]
  transfers between devices with their start and end apart: 8 -> 8, of which waited for: 8 -> 8; matrix products, arithmetic and copies ran while one was open for 0% -> 1% of each run, Pallas kernels for 0% -> 0%
where the time goes in v1:
time: 865 us; the launch traced here: 862 us
  waiting for transfers between devices  680 us (79%)
  loops' own time  63.8 us (7%)
  local copies, waits for them, and re-layouts  40.1 us (5%)
  matrix products  27.3 us (3%)
  other arithmetic  18.8 us (2%)
  starting transfers between devices  17.9 us (2%)
  between operations  14.2 us (2%)
    reduce_scatter x2, waiting for transfers between devices, local(): share_a = lax.psum_scatter(grad_a, 'col', scatter_dimension=0, tiled=True)  412 us
    all_gather x2, waiting for transfers between devices, local(): band_a = lax.all_gather(factor_a, 'col', axis=0, tiled=True)  129 us
    reduce_scatter x2, waiting for transfers between devices, local(): share_b = lax.psum_scatter(grad_b, 'row', scatter_dimension=0, tiled=True)  111 us
    another operation x2, loops' own time, local_gradients(): lax.scan(visit_slot, start, jnp.arange(slot_total, dtype=jnp.int32))  63.8 us
    all_to_all x2, waiting for transfers between devices, local(): lax.all_to_all(jnp.stack([factor_b] * lax.axis_size('row')), 'row', 0, 0)  26.2 us
    all_to_all x2, starting transfers between devices, local(): lax.all_to_all(jnp.stack([factor_b] * lax.axis_size('row')), 'row', 0, 0)  17.7 us
  transfers between devices with their start and end apart: 8, of which 8 were waited for; matrix products, arithmetic and copies ran while one was open for 1% of the time, Pallas kernels for 0%

profile of v1, /device:TPU:4, one launch (start us, length us, event | category | flops | bytes accessed | tf_op | source)
XLA Modules:
  0.0 861.8 jit_solution(87827882730778424)
XLA Ops:
  7.9 1.9 stack.4
  9.8 6.3 all-to-all-start
  16.2 13.1 %all-to-all-done = f32[16,128,128]{2,1,0:T(8,128)} async-done(((f32[16,128,128]{2,1,0:T(8,128)}), f32[16,128,128]{2,1,0:T(8,128)}, u32[]{:S(2)}, u32[]{:S(2)}) %all-to-all-start) | async-done | bytes 1048608 | tf_op jit(solution)/shard_map/all_to_all | solution.py:60
  29.3 65.0 %all-gather.3.cloned.1.call-done = f32[2048,128]{1,0:T(8,128)} async-done(((f32[128,128]{1,0:T(8,128)}), f32[2048,128]{1,0:T(8,128)}) %all-gather.3.cloned.1.call-update) | async-done | bytes 1048592 | tf_op jit(solution)/shard_map/all_gather | solution.py:58
  94.4 69.1 %while.24 = (s32[]{:T(128)}, f32[2048,128]{1,0:T(8,128)S(1)}, f32[2048,128]{1,0:T(8,128)S(1)}, s32[6]{0:T(128)S(1)}, s32[3,1,1,6]{3,2,1,0:T(1,128)S(1)}, /*index...) while((s32[]{:T(128)}, f32[2048,128]{1,0:T(8,128)S(1)}, ...), condition=%wide.region_1.2_spmd, body=%wide.region_0.1_spmd.sunk | while | flops 604667904 | bytes 5456283 | solution.py:52
  101.2 1.1 dynamic-slice_convert_fusion.4
  112.8 1.1 dynamic-slice_convert_fusion.4
  124.3 1.1 dynamic-slice_convert_fusion.4
  135.8 1.1 dynamic-slice_convert_fusion.4
  147.3 1.1 dynamic-slice_convert_fusion.4
  158.8 1.1 dynamic-slice_convert_fusion.4
  165.3 200.0 %reduce-scatter.5.cloned.1.call-done = f32[128,128]{1,0:T(8,128)} async-done(((f32[2048,128]{1,0:T(8,128)}), f32[128,128]{1,0:T(8,128)}) %reduce-scatter.5.cloned.1.call-update) | async-done | bytes 65552 | tf_op jit(solution)/shard_map/reduce_scatter | solution.py:65
  365.3 1.5 multiply_subtract_fusion.3
  366.8 57.0 %reduce-scatter.7.cloned.1.call-done = f32[128,128]{1,0:T(8,128)} async-done(((f32[2048,128]{1,0:T(8,128)}), f32[128,128]{1,0:T(8,128)}) %reduce-scatter.7.cloned.1.call-update) | async-done | bytes 65552 | tf_op jit(solution)/shard_map/reduce_scatter | solution.py:66
  424.7 1.1 stack.5
  425.7 11.4 %all-to-all-start.1 = ((f32[16,128,128]{2,1,0:T(8,128)}), f32[16,128,128]{2,1,0:T(8,128)}, u32[]{:S(2)}, u32[]{:S(2)}) async-start(f32[16,128,128]{2,1,0:T(8,128)} %stack.5), calls=%async_computation.3 | async-start | bytes 2097152 | tf_op jit(solution)/shard_map/all_to_all | solution.py:60
  437.2 13.1 %all-to-all-done.1 = f32[16,128,128]{2,1,0:T(8,128)} async-done(((f32[16,128,128]{2,1,0:T(8,128)}), f32[16,128,128]{2,1,0:T(8,128)}, u32[]{:S(2)}, u32[]{:S(2)}) %all-to-all-start.1) | async-done | bytes 1048608 | tf_op jit(solution)/shard_map/all_to_all | solution.py:60
  450.3 64.0 %all-gather.5.cloned.1.call-done = f32[2048,128]{1,0:T(8,128)} async-done(((f32[128,128]{1,0:T(8,128)}), f32[2048,128]{1,0:T(8,128)}) %all-gather.5.cloned.1.call-update) | async-done | bytes 1048592 | tf_op jit(solution)/shard_map/all_gather | solution.py:58
  514.5 69.8 %while.25 = (s32[]{:T(128)}, f32[2048,128]{1,0:T(8,128)S(1)}, f32[2048,128]{1,0:T(8,128)S(1)}, s32[6]{0:T(128)S(1)}, s32[3,1,1,6]{3,2,1,0:T(1,128)S(1)}, /*index...) while((s32[]{:T(128)}, f32[2048,128]{1,0:T(8,128)S(1)}, ...), condition=%wide.region_5.6_spmd, body=%wide.region_4.5_spmd.sunk | while | flops 604667904 | bytes 5456283 | solution.py:52
  521.4 1.1 dynamic-slice_convert_fusion.5
  585.9 53.9 %reduce-scatter.11.cloned.1.call-done = f32[128,128]{1,0:T(8,128)} async-done(((f32[2048,128]{1,0:T(8,128)}), f32[128,128]{1,0:T(8,128)}) %reduce-scatter.11.cloned.1.call-update) | async-done | bytes 65552 | tf_op jit(solution)/shard_map/reduce_scatter | solution.py:66
  639.8 1.5 multiply_subtract_fusion
  641.3 212.2 %reduce-scatter.9.cloned.1.call-done = f32[128,128]{1,0:T(8,128)} async-done(((f32[2048,128]{1,0:T(8,128)}), f32[128,128]{1,0:T(8,128)}) %reduce-scatter.9.cloned.1.call-update) | async-done | bytes 65552 | tf_op jit(solution)/shard_map/reduce_scatter | solution.py:65
  853.5 1.5 multiply_subtract_fusion.1
  (136 shorter events, 72.8 us)
Async XLA Ops:
  7.2 87.2 %copy-start.7 = (s32[3,1,1,6]{3,2,1,0:T(1,128)S(1)}, s32[3,1,1,6]{3,2,1,0:T(1,128)}, u32[]{:S(2)}) copy-start(s32[3,1,1,6]{3,2,1,0:T(1,128)} %param.11) | copy-start | bytes 220
  7.2 87.1 %all-gather.3.cloned.1.call-start = ((), (), s32[]{:S(2)}) async-start(), calls=%async_computation.6 | async-start | bytes 1114112 | tf_op jit(solution)/shard_map/all_gather | solution.py:58
  9.8 19.4 %all-to-all-start = ((f32[16,128,128]{2,1,0:T(8,128)}), f32[16,128,128]{2,1,0:T(8,128)}, u32[]{:S(2)}, u32[]{:S(2)}) async-start(f32[16,128,128]{2,1,0:T(8,128)} %stack.4), calls=%async_computation | async-start | bytes 2097152 | tf_op jit(solution)/shard_map/all_to_all | solution.py:60
  16.1 349.2 %reduce-scatter.5.cloned.1.call-start = ((), (), s32[]{:S(2)}) async-start(), calls=%async_computation.7 | async-start | bytes 1114112 | tf_op jit(solution)/shard_map/reduce_scatter | solution.py:65
  94.4 270.9 %copy-start.6 = (f32[128,128]{1,0:T(8,128)S(1)}, f32[128,128]{1,0:T(8,128)}, u32[]{:S(2)}) copy-start(f32[128,128]{1,0:T(8,128)} %param.13) | copy-start | bytes 196612
  94.4 329.4 %copy-start.5 = (f32[128,128]{1,0:T(8,128)S(1)}, f32[128,128]{1,0:T(8,128)}, u32[]{:S(2)}) copy-start(f32[128,128]{1,0:T(8,128)} %param.14) | copy-start | bytes 196612
  163.5 1.0 copy-start.2
  163.5 1.3 copy-start.3
  164.5 259.3 %reduce-scatter.7.cloned.1.call-start = ((), (), s32[]{:S(2)}) async-start(), calls=%async_computation.9 | async-start | bytes 1114112 | tf_op jit(solution)/shard_map/reduce_scatter | solution.py:66
  165.3 349.1 %all-gather.5.cloned.1.call-start = ((), (), s32[]{:S(2)}) async-start(), calls=%async_computation.8 | async-start | bytes 1114112 | tf_op jit(solution)/shard_map/all_gather | solution.py:58
  425.7 24.5 %all-to-all-start.1 = ((f32[16,128,128]{2,1,0:T(8,128)}), f32[16,128,128]{2,1,0:T(8,128)}, u32[]{:S(2)}, u32[]{:S(2)}) async-start(f32[16,128,128]{2,1,0:T(8,128)} %stack.5), calls=%async_computation.3 | async-start | bytes 2097152 | tf_op jit(solution)/shard_map/all_to_all | solution.py:60
  437.2 202.6 %reduce-scatter.11.cloned.1.call-start = ((), (), s32[]{:S(2)}) async-start(), calls=%async_computation.11 | async-start | bytes 1114112 | tf_op jit(solution)/shard_map/reduce_scatter | solution.py:66
  514.5 339.0 %copy-start.4 = (f32[128,128]{1,0:T(8,128)S(1)}, f32[128,128]{1,0:T(8,128)}, u32[]{:S(2)}) copy-start(f32[128,128]{1,0:T(8,128)} %multiply_subtract_fusion.3) | copy-start | bytes 196612
  584.3 1.0 copy-start.1
  584.3 1.3 copy-start
  585.3 268.1 %reduce-scatter.9.cloned.1.call-start = ((), (), s32[]{:S(2)}) async-start(), calls=%async_computation.10 | async-start | bytes 1114112 | tf_op jit(solution)/shard_map/reduce_scatter | solution.py:65
Sparse Core Ops, SparseCore 0:
  10.6 83.6 all-gather.2
  164.6 200.6 reduce-scatter.4
  367.8 55.9 reduce-scatter.6
  426.8 87.4 all-gather.4
  585.5 54.2 reduce-scatter.10
  643.5 209.9 reduce-scatter.8
